TPU v7x, 32 devices: a whole 2x2x4 slice. The times are simulated.
32 devices in a mesh: outer: 4 (over z), inner: 8 (over y, x, core).
Axes of the slice: x: 2, y: 2, z: 4, core: 2. Of those that a mesh axis runs over, the one named last changes fastest.
Arguments:
- queries: bfloat16 [4096, 32, 128], P(('outer', 'inner')), may hold values from -8 to 8
- key_states: bfloat16 [4096, 4, 128], P(('outer', 'inner')), may hold values from -8 to 8
- value_states: bfloat16 [4096, 4, 128], P(('outer', 'inner')), may hold values from -6 to 6
- out_grad: bfloat16 [4096, 32, 128], P(('outer', 'inner')), may hold values from -6 to 6
- bounds: int32 [3, 4096], P(None, ('outer', 'inner')), may hold values from 0 to 4095, as said below
Outputs:
- query_grad: bfloat16 [4096, 32, 128], P(('outer', 'inner'))
- key_grad: bfloat16 [4096, 4, 128], P(('outer', 'inner'))
- value_grad: bfloat16 [4096, 4, 128], P(('outer', 'inner'))
Inputs may be any that keep to these rules, and one draw needn't show every extreme that they name: For each token t, bounds[0, t] is the first token of t's document (tokens of a document are consecutive), with t - 512 < bounds[0, t] <= t; in every draw some token has t - bounds[0, t] = 511. Either bounds[1, t] = bounds[2, t] = 0, or bounds[0, t] + 2 <= bounds[1, t] < bounds[2, t] <= t.
All inputs are finite; a program needn't handle non-finite values.
Results may differ from a plain program's by a relative error of at most 0.006.
Values may be sent and summed in bfloat16 or wider, within the bound.
No kernel may reach another device: no remote copies, remote signals or barrier semaphores. Data moves between devices by JAX's collectives and lax.ppermute only.
A program may use at most 64 MiB of HBM per device.

v0:
```python
import jax
import jax.numpy as jnp
from jax import lax
from jax.sharding import PartitionSpec as P

QH = 32
KVH = 4
HD = 128
SPAN = 4


def from_behind(shard, axis, by):
    peers = lax.axis_size(axis)
    pairs = [(i, i + by) for i in range(peers) if 0 <= i + by < peers]
    return lax.ppermute(shard, axis, pairs)


def visible(query_pos, key_pos, bounds):
    doc_start = bounds[0][:, None]
    skip_low = bounds[1][:, None]
    skip_high = bounds[2][:, None]
    key_row = key_pos[None, :]
    return (
        (key_row >= doc_start)
        & (key_row <= query_pos[:, None])
        & ((key_row < skip_low) | (key_row >= skip_high))
    )


def per_device(queries, key_states, value_states, out_grad, bounds):
    token_rows = queries.shape[0]
    group_size = QH // KVH
    score_scale = HD ** (-0.5)
    my_index = lax.axis_index(("outer", "inner"))
    query_pos = my_index * token_rows + jnp.arange(token_rows, dtype=jnp.int32)
    query_four = queries.reshape(token_rows, KVH, group_size, HD)
    grad_four = out_grad.reshape(token_rows, KVH, group_size, HD)

    def seen_at(offset):
        key_pos = (my_index - offset) * token_rows + jnp.arange(token_rows, dtype=jnp.int32)
        return visible(query_pos, key_pos, bounds)

    def guarded(offset, compute):
        if offset == 0:
            return compute()
        return compute()

    def project(key_block, value_block):
        scores = (
            jnp.einsum("tkgd,skd->kgts", query_four, key_block, preferred_element_type=jnp.float32)
            * score_scale
        )
        grad_weights = jnp.einsum(
            "tkgd,skd->kgts", grad_four, value_block, preferred_element_type=jnp.float32
        )
        return (scores, grad_weights)

    def absorb(running, key_block, value_block, offset):
        row_max, row_total, weighted = running
        seen_mask = seen_at(offset)
        scores, grad_weights = project(key_block, value_block)
        new_max = jnp.maximum(row_max, jnp.max(jnp.where(seen_mask, scores, -jnp.inf), axis=-1))
        rescale = jnp.exp(row_max - new_max)
        weights = jnp.exp(jnp.where(seen_mask, scores - new_max[..., None], -jnp.inf))
        return (
            new_max,
            row_total * rescale + jnp.sum(weights, axis=-1),
            weighted * rescale + jnp.sum(weights * grad_weights, axis=-1),
        )

    stat_shape = (KVH, group_size, token_rows)
    running = (
        jnp.full(stat_shape, -jnp.inf, jnp.float32),
        jnp.zeros(stat_shape, jnp.float32),
        jnp.zeros(stat_shape, jnp.float32),
    )
    running = absorb(running, key_states, value_states, 0)
    kept = [(key_states, value_states)]
    key_now, value_now = (key_states, value_states)
    for offset in range(1, SPAN + 1):
        key_now, value_now = from_behind((key_now, value_now), ("outer", "inner"), 1)
        kept.append((key_now, value_now))
        previous = running
        running = guarded(offset, lambda: absorb(previous, key_now, value_now, offset))
    row_max, row_total, weighted = running
    log_total = row_max + jnp.log(row_total)
    row_delta = weighted / row_total

    def partial_value(key_block, value_block, offset):
        seen_mask = seen_at(offset)
        scores, grad_weights = project(key_block, value_block)
        prob = jnp.exp(jnp.where(seen_mask, scores - log_total[..., None], -jnp.inf))
        weights = prob.astype(jnp.bfloat16)
        dscore = (score_scale * prob * (grad_weights - row_delta[..., None])).astype(jnp.bfloat16)
        query_part = jnp.einsum(
            "kgts,skd->tkgd", dscore, key_block, preferred_element_type=jnp.float32
        )
        key_part = jnp.einsum(
            "kgts,tkgd->skd", dscore, query_four, preferred_element_type=jnp.float32
        )
        value_part = jnp.einsum(
            "kgts,tkgd->skd", weights, grad_four, preferred_element_type=jnp.float32
        )
        return (query_part, key_part, value_part)

    query_sum = jnp.zeros((token_rows, KVH, group_size, HD), jnp.float32)
    owned = (
        jnp.zeros((token_rows, KVH, HD), jnp.float32),
        jnp.zeros((token_rows, KVH, HD), jnp.float32),
    )
    for offset in range(SPAN + 1):
        key_now, value_now = kept[offset]
        query_part, key_part, value_part = guarded(
            offset, lambda: partial_value(key_now, value_now, offset)
        )
        query_sum = query_sum + query_part
        if offset == 0:
            owned = (key_part, value_part)
        else:
            arrived = (
                from_behind(key_part.astype(jnp.bfloat16), ("outer", "inner"), -offset).astype(
                    key_part.dtype
                ),
                from_behind(value_part.astype(jnp.bfloat16), ("outer", "inner"), -offset).astype(
                    value_part.dtype
                ),
            )
            owned = (owned[0] + arrived[0], owned[1] + arrived[1])
    query_grad = query_sum.reshape(token_rows, QH, HD).astype(jnp.bfloat16)
    return (query_grad, owned[0].astype(jnp.bfloat16), owned[1].astype(jnp.bfloat16))


def solution(mesh):
    in_specs = (
        P(("outer", "inner"), None, None),
        P(("outer", "inner"), None, None),
        P(("outer", "inner"), None, None),
        P(("outer", "inner"), None, None),
        P(None, ("outer", "inner")),
    )
    out_specs = (
        P(("outer", "inner"), None, None),
        P(("outer", "inner"), None, None),
        P(("outer", "inner"), None, None),
    )
    return jax.shard_map(
        per_device, mesh=mesh, in_specs=in_specs, out_specs=out_specs, check_vma=False
    )
```

profile of v0, /device:TPU:27, one launch (start us, length us, event | category | flops | bytes accessed | tf_op | source)
XLA Modules:
  0.0 89.1 jit_solution(15383426934858709588)
XLA Ops:
  0.7 1.0 %copy.17 = bf16[128,4,128]{2,0,1:T(8,128)(2,1)S(1)} copy(bf16[128,4,128]{2,1,0:T(4,128)(2,1)} %param.7) | data formatting | bytes 262144 | tf_op args[2]
  1.7 3.7 %collective-permute-start.4 = (bf16[128,4,128]{2,0,1:T(8,128)(2,1)S(1)}, bf16[128,4,128]{2,0,1:T(8,128)(2,1)S(1)}, u32[]{:S(2)}, u32[]{:S(2)}) collective-permute-start(bf16[128,4,128]{2,0,1:T(8,128)(2,1)S(1)} %copy.17), channel_id=1, source_target_pairs={{0,1},{1,2},{2,3},{3,4},{4,5},{5,6},{6,7},{7,8},{8,9},{9,10},{10,1... | collective-permute-start | bytes 393224 | tf_op jit(solution)/shard_map/ppermute | solution.py:15
  6.3 1.9 %collective-permute-start = (bf16[128,4,128]{2,0,1:T(8,128)(2,1)S(1)}, bf16[128,4,128]{2,0,1:T(8,128)(2,1)S(1)}, u32[]{:S(2)}, u32[]{:S(2)}) collective-permute-start(bf16[128,4,128]{2,0,1:T(8,128)(2,1)S(1)} %copy.10), channel_id=1, source_target_pairs={{0,1},{1,2},{2,3},{3,4},{4,5},{5,6},{6,7},{7,8},{8,9},{9,10},{10,1... | collective-permute-start | bytes 393224 | tf_op jit(solution)/shard_map/ppermute | solution.py:15
  9.2 2.0 %fusion.35 = (f32[4,8,128]{2,1,0:T(8,128)S(1)}, f32[4,128,128,8]{2,1,3,0:T(8,128)S(1)}) fusion(pred[128,128]{0,1:T(8,128)(4,1)S(1)} %get-tuple-element.31, bf16[128,4,8,128]{3,2,1,0:T(8,128)(2,1)} %bitcast.346, bf16[128,4,128,1]{2,1,0,3:T(4,128)(2,1)} %bitcast.357), kind=kOutput, calls=%fused_computation.60 | convolution fusion | flops 135786496 | bytes 3309568 | tf_op jit(solution)/shard_map/tkgd,skd->kgts/dot_general | solution.py:50
  11.3 1.0 %fusion.41 = (f32[4,8,128]{2,1,0:T(8,128)S(1)}, f32[4,8,128]{2,1,0:T(8,128)S(1)}, f32[4,128,128,8]{2,1,3,0:T(8,128)S(1)}) fusion(f32[4,128,128,8]{2,1,3,0:T(8,128)S(1)} %get-tuple-element.42, f32[4,8,128]{2,1,0:T(8,128)S(1)} %get-tuple-element.41, pred[128,128]{0,1:T(8,128)(4,1)S(1)} %get-tuple-element.31, bf16[128,4,8,128]{3,2,1,0:T(8,128)(2,1)S(1)} %bitcast.336, ...), kind=kOutput, calls=%fused_computation.67 | convolution fusion | flops 137355264 | bytes 5439488 | tf_op jit(solution)/shard_map/tkgd,skd->kgts/dot_general | solution.py:53
  12.3 3.5 %collective-permute-start.5 = (bf16[128,4,128]{2,0,1:T(8,128)(2,1)S(1)}, bf16[128,4,128]{2,0,1:T(8,128)(2,1)S(1)}, u32[]{:S(2)}, u32[]{:S(2)}) collective-permute-start(bf16[128,4,128]{2,0,1:T(8,128)(2,1)S(1)} %collective-permute-done.4), channel_id=1, source_target_pairs={{0,1},{1,2},{2,3},{3,4},{4,5},{5,6},{6,7},{7,8},{8,9},{9,10},{10,1... | collective-permute-start | bytes 393224 | tf_op jit(solution)/shard_map/ppermute | solution.py:15
  15.8 1.9 %collective-permute-start.1 = (bf16[128,4,128]{2,0,1:T(8,128)(2,1)S(1)}, bf16[128,4,128]{2,0,1:T(8,128)(2,1)S(1)}, u32[]{:S(2)}, u32[]{:S(2)}) collective-permute-start(bf16[128,4,128]{2,0,1:T(8,128)(2,1)S(1)} %collective-permute-done), channel_id=1, source_target_pairs={{0,1},{1,2},{2,3},{3,4},{4,5},{5,6},{6,7},{7,8},{8,9},{9,10},{10,1... | collective-permute-start | bytes 393224 | tf_op jit(solution)/shard_map/ppermute | solution.py:15
  18.4 4.5 %collective-permute-start.6 = (bf16[128,4,128]{2,0,1:T(8,128)(2,1)S(1)}, bf16[128,4,128]{2,0,1:T(8,128)(2,1)S(1)}, u32[]{:S(2)}, u32[]{:S(2)}) collective-permute-start(bf16[128,4,128]{2,0,1:T(8,128)(2,1)S(1)} %collective-permute-done.5), channel_id=1, source_target_pairs={{0,1},{1,2},{2,3},{3,4},{4,5},{5,6},{6,7},{7,8},{8,9},{9,10},{10,1... | collective-permute-start | bytes 393224 | tf_op jit(solution)/shard_map/ppermute | solution.py:15
  23.0 1.9 %collective-permute-start.2 = (bf16[128,4,128]{2,0,1:T(8,128)(2,1)S(1)}, bf16[128,4,128]{2,0,1:T(8,128)(2,1)S(1)}, u32[]{:S(2)}, u32[]{:S(2)}) collective-permute-start(bf16[128,4,128]{2,0,1:T(8,128)(2,1)S(1)} %collective-permute-done.1), channel_id=1, source_target_pairs={{0,1},{1,2},{2,3},{3,4},{4,5},{5,6},{6,7},{7,8},{8,9},{9,10},{10,1... | collective-permute-start | bytes 393224 | tf_op jit(solution)/shard_map/ppermute | solution.py:15
  25.6 4.5 %collective-permute-start.7 = (bf16[128,4,128]{2,0,1:T(8,128)(2,1)S(1)}, bf16[128,4,128]{2,0,1:T(8,128)(2,1)S(1)}, u32[]{:S(2)}, u32[]{:S(2)}) collective-permute-start(bf16[128,4,128]{2,0,1:T(8,128)(2,1)S(1)} %collective-permute-done.6), channel_id=1, source_target_pairs={{0,1},{1,2},{2,3},{3,4},{4,5},{5,6},{6,7},{7,8},{8,9},{9,10},{10,1... | collective-permute-start | bytes 393224 | tf_op jit(solution)/shard_map/ppermute | solution.py:15
  30.2 2.1 %collective-permute-start.3 = (bf16[128,4,128]{2,0,1:T(8,128)(2,1)S(1)}, bf16[128,4,128]{2,0,1:T(8,128)(2,1)S(1)}, u32[]{:S(2)}, u32[]{:S(2)}) collective-permute-start(bf16[128,4,128]{2,0,1:T(8,128)(2,1)S(1)} %collective-permute-done.2), channel_id=1, source_target_pairs={{0,1},{1,2},{2,3},{3,4},{4,5},{5,6},{6,7},{7,8},{8,9},{9,10},{10,1... | collective-permute-start | bytes 393224 | tf_op jit(solution)/shard_map/ppermute | solution.py:15
  32.9 1.1 %collective-permute-done.3 = bf16[128,4,128]{2,0,1:T(8,128)(2,1)S(1)} collective-permute-done((bf16[128,4,128]{2,0,1:T(8,128)(2,1)S(1)}, bf16[128,4,128]{2,0,1:T(8,128)(2,1)S(1)}, u32[]{:S(2)}, u32[]{:S(2)}) %collective-permute-start.3) | collective-permute-done | bytes 131104 | tf_op jit(solution)/shard_map/ppermute | solution.py:15
  34.7 1.0 %fusion.47 = (f32[4,8,128]{2,1,0:T(8,128)S(1)}, f32[4,8,128]{2,1,0:T(8,128)S(1)}, f32[4,128,128,8]{2,1,3,0:T(8,128)S(1)}) fusion(f32[4,128,128,8]{2,1,3,0:T(8,128)S(1)} %get-tuple-element.38, f32[4,8,128]{2,1,0:T(8,128)S(1)} %get-tuple-element.17, pred[128,128]{0,1:T(8,128)(4,1)S(1)} %get-tuple-element.29, bf16[128,4,8,128]{3,2,1,0:T(8,128)(2,1)S(1)} %bitcast.343, ...), kind=kOutput, calls=%fused_computation.73 | convolution fusion | flops 137355264 | bytes 5439488 | tf_op jit(solution)/shard_map/tkgd,skd->kgts/dot_general | solution.py:53
  35.7 1.0 %fusion.45 = (f32[4,8,128]{2,1,0:T(8,128)S(1)}, f32[4,8,128]{2,1,0:T(8,128)S(1)}, f32[4,128,128,8]{2,1,3,0:T(8,128)S(1)}) fusion(f32[4,128,128,8]{2,1,3,0:T(8,128)S(1)} %get-tuple-element.40, f32[4,8,128]{2,1,0:T(8,128)S(1)} %get-tuple-element.18, pred[128,128]{0,1:T(8,128)(4,1)S(1)} %get-tuple-element.28, bf16[128,4,8,128]{3,2,1,0:T(8,128)(2,1)S(1)} %bitcast.344, ...), kind=kOutput, calls=%fused_computation.71 | convolution fusion | flops 137355264 | bytes 5439488 | tf_op jit(solution)/shard_map/tkgd,skd->kgts/dot_general | solution.py:53
  36.8 1.0 %fusion.43 = (f32[4,8,128]{2,1,0:T(8,128)S(1)}, f32[4,8,128]{2,1,0:T(8,128)S(1)}, f32[4,128,128,8]{2,1,3,0:T(8,128)S(1)}) fusion(f32[4,128,128,8]{2,1,3,0:T(8,128)S(1)} %get-tuple-element.44, f32[4,8,128]{2,1,0:T(8,128)S(1)} %get-tuple-element.19, pred[128,128]{0,1:T(8,128)(4,1)S(1)} %get-tuple-element.27, bf16[128,4,8,128]{3,2,1,0:T(8,128)(2,1)S(1)} %bitcast.345, ...), kind=kOutput, calls=%fused_computation.69 | convolution fusion | flops 137355264 | bytes 5439488 | tf_op jit(solution)/shard_map/tkgd,skd->kgts/dot_general | solution.py:53
  37.8 1.0 %fusion.49 = (f32[4,8,128]{2,1,0:T(8,128)S(1)}, f32[4,8,128]{2,1,0:T(8,128)S(1)}, f32[4,128,128,8]{2,1,3,0:T(8,128)S(1)}) fusion(f32[4,128,128,8]{2,1,3,0:T(8,128)S(1)} %get-tuple-element.36, f32[4,8,128]{2,1,0:T(8,128)S(1)} %get-tuple-element.16, pred[128,128]{0,1:T(8,128)(4,1)S(1)} %get-tuple-element.30, bf16[128,4,8,128]{3,2,1,0:T(8,128)(2,1)S(1)} %bitcast.342, ...), kind=kOutput, calls=%fused_computation.75 | convolution fusion | flops 137355264 | bytes 5439488 | tf_op jit(solution)/shard_map/tkgd,skd->kgts/dot_general | solution.py:53
  38.9 1.5 %fusion.61 = bf16[128,4,128]{2,0,1:T(8,128)(2,1)} fusion(f32[4,128,128,8]{2,1,3,0:T(8,128)S(1)} %get-tuple-element.44, f32[4,8,128]{2,1,0:T(8,128)S(1)} %get-tuple-element.20, pred[128,128]{0,1:T(8,128)(4,1)S(1)} %get-tuple-element.27, bf16[128,4,8,128]{3,2,1,0:T(8,128)(2,1)S(1)} %bitcast.340), kind=kOutput, calls=%fused_computation.97 | convolution fusion | flops 136380416 | bytes 3309568 | tf_op jit(solution)/shard_map/kgts,tkgd->skd/dot_general | solution.py:101
  40.4 1.6 %fusion.60 = bf16[128,4,128]{2,0,1:T(8,128)(2,1)} fusion(f32[4,128,128,8]{2,1,3,0:T(8,128)S(1)} %get-tuple-element.40, f32[4,8,128]{2,1,0:T(8,128)S(1)} %get-tuple-element.20, pred[128,128]{0,1:T(8,128)(4,1)S(1)} %get-tuple-element.28, bf16[128,4,8,128]{3,2,1,0:T(8,128)(2,1)S(1)} %bitcast.339), kind=kOutput, calls=%fused_computation.96 | convolution fusion | flops 136380416 | bytes 3309568 | tf_op jit(solution)/shard_map/kgts,tkgd->skd/dot_general | solution.py:101
  42.0 1.6 %fusion.59 = bf16[128,4,128]{2,0,1:T(8,128)(2,1)} fusion(f32[4,128,128,8]{2,1,3,0:T(8,128)S(1)} %get-tuple-element.38, f32[4,8,128]{2,1,0:T(8,128)S(1)} %get-tuple-element.20, pred[128,128]{0,1:T(8,128)(4,1)S(1)} %get-tuple-element.29, bf16[128,4,8,128]{3,2,1,0:T(8,128)(2,1)S(1)} %bitcast.338), kind=kOutput, calls=%fused_computation.95 | convolution fusion | flops 136380416 | bytes 3309568 | tf_op jit(solution)/shard_map/kgts,tkgd->skd/dot_general | solution.py:101
  43.5 1.6 %fusion.58 = bf16[128,4,128]{2,0,1:T(8,128)(2,1)} fusion(f32[4,128,128,8]{2,1,3,0:T(8,128)S(1)} %get-tuple-element.36, f32[4,8,128]{2,1,0:T(8,128)S(1)} %get-tuple-element.20, pred[128,128]{0,1:T(8,128)(4,1)S(1)} %get-tuple-element.30, bf16[128,4,8,128]{3,2,1,0:T(8,128)(2,1)S(1)} %bitcast.337), kind=kOutput, calls=%fused_computation.94 | convolution fusion | flops 136380416 | bytes 3309568 | tf_op jit(solution)/shard_map/kgts,tkgd->skd/dot_general | solution.py:101
  45.1 3.3 %fusion.2 = (bf16[4,8,128,128]{2,3,1,0:T(8,128)(2,1)S(1)}, bf16[4,8,128,128]{2,3,1,0:T(8,128)(2,1)S(1)}, bf16[4,8,128,128]{2,3,1,0:T(8,128)(2,1)S(1)}, bf16[4,8,...) fusion(f32[4,128,128,8]{2,1,3,0:T(8,128)S(1)} %get-tuple-element.45, f32[4,128,128,8]{2,1,3,0:T(8,128)S(1)} %get-tuple-element.36, ...), kind=kLoop, calls=%fused_computation.4 | loop fusion | flops 18350080 | bytes 26329088 | tf_op jit(solution)/shard_map/convert_element_type | solution.py:94
  50.8 7.0 %collective-permute-start.10 = (bf16[128,4,128]{2,0,1:T(8,128)(2,1)S(1)}, bf16[128,4,128]{2,0,1:T(8,128)(2,1)S(1)}, u32[]{:S(2)}, u32[]{:S(2)}) collective-permute-start(bf16[128,4,128]{2,0,1:T(8,128)(2,1)S(1)} %fusion.63), channel_id=1, source_target_pairs={{3,0},{4,1},{5,2},{6,3},{7,4},{8,5},{9,6},{10,7},{11,8},{12,9},{13... | collective-permute-start | bytes 393224 | tf_op jit(solution)/shard_map/ppermute | solution.py:15
  57.8 1.9 %collective-permute-start.9 = (bf16[128,4,128]{2,0,1:T(8,128)(2,1)S(1)}, bf16[128,4,128]{2,0,1:T(8,128)(2,1)S(1)}, u32[]{:S(2)}, u32[]{:S(2)}) collective-permute-start(bf16[128,4,128]{2,0,1:T(8,128)(2,1)S(1)} %fusion.64), channel_id=1, source_target_pairs={{2,0},{3,1},{4,2},{5,3},{6,4},{7,5},{8,6},{9,7},{10,8},{11,9},{12,... | collective-permute-start | bytes 393224 | tf_op jit(solution)/shard_map/ppermute | solution.py:15
  59.8 2.3 %collective-permute-start.8 = (bf16[128,4,128]{2,0,1:T(8,128)(2,1)S(1)}, bf16[128,4,128]{2,0,1:T(8,128)(2,1)S(1)}, u32[]{:S(2)}, u32[]{:S(2)}) collective-permute-start(bf16[128,4,128]{2,0,1:T(8,128)(2,1)S(1)} %fusion.65), channel_id=1, source_target_pairs={{1,0},{2,1},{3,2},{4,3},{5,4},{6,5},{7,6},{8,7},{9,8},{10,9},{11,1... | collective-permute-start | bytes 393224 | tf_op jit(solution)/shard_map/ppermute | solution.py:15
  62.1 1.9 %collective-permute-start.11 = (bf16[128,4,128]{2,0,1:T(8,128)(2,1)S(1)}, bf16[128,4,128]{2,0,1:T(8,128)(2,1)S(1)}, u32[]{:S(2)}, u32[]{:S(2)}) collective-permute-start(bf16[128,4,128]{2,0,1:T(8,128)(2,1)S(1)} %fusion.62), channel_id=1, source_target_pairs={{4,0},{5,1},{6,2},{7,3},{8,4},{9,5},{10,6},{11,7},{12,8},{13,9},{1... | collective-permute-start | bytes 393224 | tf_op jit(solution)/shard_map/ppermute | solution.py:15
  64.0 3.2 %collective-permute-start.15 = (bf16[128,4,128]{2,0,1:T(8,128)(2,1)S(1)}, bf16[128,4,128]{2,0,1:T(8,128)(2,1)S(1)}, u32[]{:S(2)}, u32[]{:S(2)}) collective-permute-start(bf16[128,4,128]{2,0,1:T(8,128)(2,1)S(1)} %copy-done.9), channel_id=1, source_target_pairs={{4,0},{5,1},{6,2},{7,3},{8,4},{9,5},{10,6},{11,7},{12,8},{13,9},{1... | collective-permute-start | bytes 393224 | tf_op jit(solution)/shard_map/ppermute | solution.py:15
  70.5 1.6 %copy.38 = bf16[128,32,128]{2,1,0:T(8,128)(2,1)} copy(bf16[128,32,128]{2,0,1:T(8,128)(2,1)S(1)} %bitcast.356) | data formatting | bytes 2097152
  72.2 3.3 %collective-permute-start.14 = (bf16[128,4,128]{2,0,1:T(8,128)(2,1)S(1)}, bf16[128,4,128]{2,0,1:T(8,128)(2,1)S(1)}, u32[]{:S(2)}, u32[]{:S(2)}) collective-permute-start(bf16[128,4,128]{2,0,1:T(8,128)(2,1)S(1)} %copy-done.8), channel_id=1, source_target_pairs={{3,0},{4,1},{5,2},{6,3},{7,4},{8,5},{9,6},{10,7},{11,8},{12,9},{13... | collective-permute-start | bytes 393224 | tf_op jit(solution)/shard_map/ppermute | solution.py:15
  75.5 4.7 %collective-permute-start.13 = (bf16[128,4,128]{2,0,1:T(8,128)(2,1)S(1)}, bf16[128,4,128]{2,0,1:T(8,128)(2,1)S(1)}, u32[]{:S(2)}, u32[]{:S(2)}) collective-permute-start(bf16[128,4,128]{2,0,1:T(8,128)(2,1)S(1)} %copy-done.7), channel_id=1, source_target_pairs={{2,0},{3,1},{4,2},{5,3},{6,4},{7,5},{8,6},{9,7},{10,8},{11,9},{12,... | collective-permute-start | bytes 393224 | tf_op jit(solution)/shard_map/ppermute | solution.py:15
  80.2 1.9 %collective-permute-start.12 = (bf16[128,4,128]{2,0,1:T(8,128)(2,1)S(1)}, bf16[128,4,128]{2,0,1:T(8,128)(2,1)S(1)}, u32[]{:S(2)}, u32[]{:S(2)}) collective-permute-start(bf16[128,4,128]{2,0,1:T(8,128)(2,1)S(1)} %copy-done.6), channel_id=1, source_target_pairs={{1,0},{2,1},{3,2},{4,3},{5,4},{6,5},{7,6},{8,7},{9,8},{10,9},{11,1... | collective-permute-start | bytes 393224 | tf_op jit(solution)/shard_map/ppermute | solution.py:15
  83.5 3.9 %collective-permute-done.12 = bf16[128,4,128]{2,0,1:T(8,128)(2,1)S(1)} collective-permute-done((bf16[128,4,128]{2,0,1:T(8,128)(2,1)S(1)}, bf16[128,4,128]{2,0,1:T(8,128)(2,1)S(1)}, u32[]{:S(2)}, u32[]{:S(2)}) %collective-permute-start.12) | collective-permute-done | bytes 131104 | tf_op jit(solution)/shard_map/ppermute | solution.py:15
  87.4 0.9 %add_convert_fusion.1 = bf16[128,4,128]{2,0,1:T(8,128)(2,1)S(1)} fusion(bf16[128,4,128]{2,0,1:T(8,128)(2,1)S(1)} %collective-permute-done.15, bf16[128,4,128]{2,0,1:T(8,128)(2,1)S(1)} %collective-permute-done.14, bf16[128,4,128]{2,0,1:T(8,128)(2,1)S(1)} %collective-permute-done.13, bf16[128,4,128]{2,0,1:T(8,128)(2,1)S(1)} %collective-permute-done.12, ...), kind=kOutput, calls=%fused_computation.122 | convolution fusion | flops 136904704 | bytes 3833856 | tf_op jit(solution)/shard_map/kgts,tkgd->skd/dot_general | solution.py:101
  (58 shorter events, 12.4 us)
Async XLA Ops:
  0.6 10.6 %copy-start = (bf16[128,32,128]{2,1,0:T(8,128)(2,1)S(1)}, bf16[128,32,128]{2,1,0:T(8,128)(2,1)}, u32[]{:S(2)}) copy-start(bf16[128,32,128]{2,1,0:T(8,128)(2,1)} %param.8) | copy-start | bytes 3145732
  0.6 10.6 %copy-start.3 = (bf16[128,4,128]{2,1,0:T(4,128)(2,1)S(1)}, bf16[128,4,128]{2,1,0:T(4,128)(2,1)}, u32[]{:S(2)}) copy-start(bf16[128,4,128]{2,1,0:T(4,128)(2,1)} %param.7) | copy-start | bytes 393220
  1.7 10.6 %collective-permute-start.4 = (bf16[128,4,128]{2,0,1:T(8,128)(2,1)S(1)}, bf16[128,4,128]{2,0,1:T(8,128)(2,1)S(1)}, u32[]{:S(2)}, u32[]{:S(2)}) collective-permute-start(bf16[128,4,128]{2,0,1:T(8,128)(2,1)S(1)} %copy.17), channel_id=1, source_target_pairs={{0,1},{1,2},{2,3},{3,4},{4,5},{5,6},{6,7},{7,8},{8,9},{9,10},{10,1... | collective-permute-start | bytes 393224 | tf_op jit(solution)/shard_map/ppermute | solution.py:15
  6.3 9.5 %collective-permute-start = (bf16[128,4,128]{2,0,1:T(8,128)(2,1)S(1)}, bf16[128,4,128]{2,0,1:T(8,128)(2,1)S(1)}, u32[]{:S(2)}, u32[]{:S(2)}) collective-permute-start(bf16[128,4,128]{2,0,1:T(8,128)(2,1)S(1)} %copy.10), channel_id=1, source_target_pairs={{0,1},{1,2},{2,3},{3,4},{4,5},{5,6},{6,7},{7,8},{8,9},{9,10},{10,1... | collective-permute-start | bytes 393224 | tf_op jit(solution)/shard_map/ppermute | solution.py:15
  11.2 6.5 %copy-start.1 = (bf16[128,32,128]{2,1,0:T(8,128)(2,1)S(1)}, bf16[128,32,128]{2,1,0:T(8,128)(2,1)}, u32[]{:S(2)}) copy-start(bf16[128,32,128]{2,1,0:T(8,128)(2,1)} %param.5) | copy-start | bytes 3145732
  12.3 6.1 %collective-permute-start.5 = (bf16[128,4,128]{2,0,1:T(8,128)(2,1)S(1)}, bf16[128,4,128]{2,0,1:T(8,128)(2,1)S(1)}, u32[]{:S(2)}, u32[]{:S(2)}) collective-permute-start(bf16[128,4,128]{2,0,1:T(8,128)(2,1)S(1)} %collective-permute-done.4), channel_id=1, source_target_pairs={{0,1},{1,2},{2,3},{3,4},{4,5},{5,6},{6,7},{7,8},{8,9},{9,10},{10,1... | collective-permute-start | bytes 393224 | tf_op jit(solution)/shard_map/ppermute | solution.py:15
  15.8 7.2 %collective-permute-start.1 = (bf16[128,4,128]{2,0,1:T(8,128)(2,1)S(1)}, bf16[128,4,128]{2,0,1:T(8,128)(2,1)S(1)}, u32[]{:S(2)}, u32[]{:S(2)}) collective-permute-start(bf16[128,4,128]{2,0,1:T(8,128)(2,1)S(1)} %collective-permute-done), channel_id=1, source_target_pairs={{0,1},{1,2},{2,3},{3,4},{4,5},{5,6},{6,7},{7,8},{8,9},{9,10},{10,1... | collective-permute-start | bytes 393224 | tf_op jit(solution)/shard_map/ppermute | solution.py:15
  18.4 7.2 %collective-permute-start.6 = (bf16[128,4,128]{2,0,1:T(8,128)(2,1)S(1)}, bf16[128,4,128]{2,0,1:T(8,128)(2,1)S(1)}, u32[]{:S(2)}, u32[]{:S(2)}) collective-permute-start(bf16[128,4,128]{2,0,1:T(8,128)(2,1)S(1)} %collective-permute-done.5), channel_id=1, source_target_pairs={{0,1},{1,2},{2,3},{3,4},{4,5},{5,6},{6,7},{7,8},{8,9},{9,10},{10,1... | collective-permute-start | bytes 393224 | tf_op jit(solution)/shard_map/ppermute | solution.py:15
  23.0 7.2 %collective-permute-start.2 = (bf16[128,4,128]{2,0,1:T(8,128)(2,1)S(1)}, bf16[128,4,128]{2,0,1:T(8,128)(2,1)S(1)}, u32[]{:S(2)}, u32[]{:S(2)}) collective-permute-start(bf16[128,4,128]{2,0,1:T(8,128)(2,1)S(1)} %collective-permute-done.1), channel_id=1, source_target_pairs={{0,1},{1,2},{2,3},{3,4},{4,5},{5,6},{6,7},{7,8},{8,9},{9,10},{10,1... | collective-permute-start | bytes 393224 | tf_op jit(solution)/shard_map/ppermute | solution.py:15
  25.6 12.2 %collective-permute-start.7 = (bf16[128,4,128]{2,0,1:T(8,128)(2,1)S(1)}, bf16[128,4,128]{2,0,1:T(8,128)(2,1)S(1)}, u32[]{:S(2)}, u32[]{:S(2)}) collective-permute-start(bf16[128,4,128]{2,0,1:T(8,128)(2,1)S(1)} %collective-permute-done.6), channel_id=1, source_target_pairs={{0,1},{1,2},{2,3},{3,4},{4,5},{5,6},{6,7},{7,8},{8,9},{9,10},{10,1... | collective-permute-start | bytes 393224 | tf_op jit(solution)/shard_map/ppermute | solution.py:15
  30.2 3.9 %collective-permute-start.3 = (bf16[128,4,128]{2,0,1:T(8,128)(2,1)S(1)}, bf16[128,4,128]{2,0,1:T(8,128)(2,1)S(1)}, u32[]{:S(2)}, u32[]{:S(2)}) collective-permute-start(bf16[128,4,128]{2,0,1:T(8,128)(2,1)S(1)} %collective-permute-done.2), channel_id=1, source_target_pairs={{0,1},{1,2},{2,3},{3,4},{4,5},{5,6},{6,7},{7,8},{8,9},{9,10},{10,1... | collective-permute-start | bytes 393224 | tf_op jit(solution)/shard_map/ppermute | solution.py:15
  34.0 1.7 %copy-start.4 = (bf16[128,4,128]{2,0,1:T(8,128)(2,1)}, bf16[128,4,128]{2,0,1:T(8,128)(2,1)S(1)}, u32[]{:S(2)}) copy-start(bf16[128,4,128]{2,0,1:T(8,128)(2,1)S(1)} %collective-permute-done.3) | copy-start | bytes 393220
  49.6 14.4 %copy-start.9 = (bf16[128,4,128]{2,0,1:T(8,128)(2,1)S(1)}, bf16[128,4,128]{2,0,1:T(8,128)(2,1)}, u32[]{:S(2)}) copy-start(bf16[128,4,128]{2,0,1:T(8,128)(2,1)} %fusion.58) | copy-start | bytes 393220
  49.6 17.6 %copy-start.2 = (bf16[128,4,128]{2,1,0:T(4,128)(2,1)S(1)}, bf16[128,4,128]{2,1,0:T(4,128)(2,1)}, u32[]{:S(2)}) copy-start(bf16[128,4,128]{2,1,0:T(4,128)(2,1)} %param.6) | copy-start | bytes 393220
  50.8 21.3 %collective-permute-start.10 = (bf16[128,4,128]{2,0,1:T(8,128)(2,1)S(1)}, bf16[128,4,128]{2,0,1:T(8,128)(2,1)S(1)}, u32[]{:S(2)}, u32[]{:S(2)}) collective-permute-start(bf16[128,4,128]{2,0,1:T(8,128)(2,1)S(1)} %fusion.63), channel_id=1, source_target_pairs={{3,0},{4,1},{5,2},{6,3},{7,4},{8,5},{9,6},{10,7},{11,8},{12,9},{13... | collective-permute-start | bytes 393224 | tf_op jit(solution)/shard_map/ppermute | solution.py:15
  57.8 17.6 %collective-permute-start.9 = (bf16[128,4,128]{2,0,1:T(8,128)(2,1)S(1)}, bf16[128,4,128]{2,0,1:T(8,128)(2,1)S(1)}, u32[]{:S(2)}, u32[]{:S(2)}) collective-permute-start(bf16[128,4,128]{2,0,1:T(8,128)(2,1)S(1)} %fusion.64), channel_id=1, source_target_pairs={{2,0},{3,1},{4,2},{5,3},{6,4},{7,5},{8,6},{9,7},{10,8},{11,9},{12,... | collective-permute-start | bytes 393224 | tf_op jit(solution)/shard_map/ppermute | solution.py:15
  59.8 20.4 %collective-permute-start.8 = (bf16[128,4,128]{2,0,1:T(8,128)(2,1)S(1)}, bf16[128,4,128]{2,0,1:T(8,128)(2,1)S(1)}, u32[]{:S(2)}, u32[]{:S(2)}) collective-permute-start(bf16[128,4,128]{2,0,1:T(8,128)(2,1)S(1)} %fusion.65), channel_id=1, source_target_pairs={{1,0},{2,1},{3,2},{4,3},{5,4},{6,5},{7,6},{8,7},{9,8},{10,9},{11,1... | collective-permute-start | bytes 393224 | tf_op jit(solution)/shard_map/ppermute | solution.py:15
  62.1 20.0 %collective-permute-start.11 = (bf16[128,4,128]{2,0,1:T(8,128)(2,1)S(1)}, bf16[128,4,128]{2,0,1:T(8,128)(2,1)S(1)}, u32[]{:S(2)}, u32[]{:S(2)}) collective-permute-start(bf16[128,4,128]{2,0,1:T(8,128)(2,1)S(1)} %fusion.62), channel_id=1, source_target_pairs={{4,0},{5,1},{6,2},{7,3},{8,4},{9,5},{10,6},{11,7},{12,8},{13,9},{1... | collective-permute-start | bytes 393224 | tf_op jit(solution)/shard_map/ppermute | solution.py:15
  64.0 19.5 %collective-permute-start.15 = (bf16[128,4,128]{2,0,1:T(8,128)(2,1)S(1)}, bf16[128,4,128]{2,0,1:T(8,128)(2,1)S(1)}, u32[]{:S(2)}, u32[]{:S(2)}) collective-permute-start(bf16[128,4,128]{2,0,1:T(8,128)(2,1)S(1)} %copy-done.9), channel_id=1, source_target_pairs={{4,0},{5,1},{6,2},{7,3},{8,4},{9,5},{10,6},{11,7},{12,8},{13,9},{1... | collective-permute-start | bytes 393224 | tf_op jit(solution)/shard_map/ppermute | solution.py:15
  68.9 0.9 %copy-start.5 = (bf16[128,4,128]{2,0,1:T(8,128)(2,1)S(1)}, bf16[128,4,128]{2,0,1:T(8,128)(2,1)}, u32[]{:S(2)}) copy-start(bf16[128,4,128]{2,0,1:T(8,128)(2,1)} %copy-done.4) | copy-start | bytes 393220
  70.5 1.7 %copy-start.8 = (bf16[128,4,128]{2,0,1:T(8,128)(2,1)S(1)}, bf16[128,4,128]{2,0,1:T(8,128)(2,1)}, u32[]{:S(2)}) copy-start(bf16[128,4,128]{2,0,1:T(8,128)(2,1)} %fusion.59) | copy-start | bytes 393220
  70.5 5.0 %copy-start.7 = (bf16[128,4,128]{2,0,1:T(8,128)(2,1)S(1)}, bf16[128,4,128]{2,0,1:T(8,128)(2,1)}, u32[]{:S(2)}) copy-start(bf16[128,4,128]{2,0,1:T(8,128)(2,1)} %fusion.60) | copy-start | bytes 393220
  70.5 9.7 %copy-start.6 = (bf16[128,4,128]{2,0,1:T(8,128)(2,1)S(1)}, bf16[128,4,128]{2,0,1:T(8,128)(2,1)}, u32[]{:S(2)}) copy-start(bf16[128,4,128]{2,0,1:T(8,128)(2,1)} %fusion.61) | copy-start | bytes 393220
  72.2 11.3 %collective-permute-start.14 = (bf16[128,4,128]{2,0,1:T(8,128)(2,1)S(1)}, bf16[128,4,128]{2,0,1:T(8,128)(2,1)S(1)}, u32[]{:S(2)}, u32[]{:S(2)}) collective-permute-start(bf16[128,4,128]{2,0,1:T(8,128)(2,1)S(1)} %copy-done.8), channel_id=1, source_target_pairs={{3,0},{4,1},{5,2},{6,3},{7,4},{8,5},{9,6},{10,7},{11,8},{12,9},{13... | collective-permute-start | bytes 393224 | tf_op jit(solution)/shard_map/ppermute | solution.py:15
  75.5 8.0 %collective-permute-start.13 = (bf16[128,4,128]{2,0,1:T(8,128)(2,1)S(1)}, bf16[128,4,128]{2,0,1:T(8,128)(2,1)S(1)}, u32[]{:S(2)}, u32[]{:S(2)}) collective-permute-start(bf16[128,4,128]{2,0,1:T(8,128)(2,1)S(1)} %copy-done.7), channel_id=1, source_target_pairs={{2,0},{3,1},{4,2},{5,3},{6,4},{7,5},{8,6},{9,7},{10,8},{11,9},{12,... | collective-permute-start | bytes 393224 | tf_op jit(solution)/shard_map/ppermute | solution.py:15
  80.2 7.2 %collective-permute-start.12 = (bf16[128,4,128]{2,0,1:T(8,128)(2,1)S(1)}, bf16[128,4,128]{2,0,1:T(8,128)(2,1)S(1)}, u32[]{:S(2)}, u32[]{:S(2)}) collective-permute-start(bf16[128,4,128]{2,0,1:T(8,128)(2,1)S(1)} %copy-done.6), channel_id=1, source_target_pairs={{1,0},{2,1},{3,2},{4,3},{5,4},{6,5},{7,6},{8,7},{9,8},{10,9},{11,1... | collective-permute-start | bytes 393224 | tf_op jit(solution)/shard_map/ppermute | solution.py:15
where the time goes:
time: 89.7 us; the launch traced here: 89.1 us
  starting transfers between devices  50.4 us (56%)
  matrix products  22.7 us (25%)
  local copies, waits for them, and re-layouts  6.31 us (7%)
  waiting for transfers between devices  4.97 us (6%)
  other arithmetic  3.55 us (4%)
  between operations  1.18 us (1%)
    ppermute x16, starting transfers between devices, from_behind(): return lax.ppermute(shard, axis, pairs)  50.4 us
    dot_general x5, matrix products, partial_value(): jnp.einsum('kgts,tkgd->skd', weights, grad_four, preferred_element_type=j...  7.13 us
    unnamed x25, local copies, waits for them, and re-layouts  5.51 us
    dot_general x5, matrix products, project(): jnp.einsum('tkgd,skd->kgts', grad_four, value_block, preferred_element_ty...  5.08 us
    ppermute x16, waiting for transfers between devices, from_behind(): return lax.ppermute(shard, axis, pairs)  4.97 us
    dot_general x5, matrix products, project(): jnp.einsum('tkgd,skd->kgts', query_four, key_block, preferred_element_typ...  4.66 us
    convert_element_type x1, other arithmetic, partial_value(): (score_scale * prob * (grad_weights - row_delta[..., None])).astype(jnp.b...  3.32 us
    dot_general x5, matrix products, partial_value(): jnp.einsum('kgts,tkgd->skd', dscore, query_four, preferred_element_type=j...  2.97 us
  transfers between devices with their start and end apart: 16, of which 2 were waited for; matrix products, arithmetic and copies ran while one was open for 18% of the time, Pallas kernels for 0%

commit v1 on v0

v1 whole, which is shorter than its diff:
```python
import math

import jax
import jax.numpy as jnp
from jax import lax
from jax.experimental import pallas as pl
from jax.experimental.pallas import tpu as pltpu
from jax.sharding import PartitionSpec as P

AXES = ("outer", "inner")
SPAN = 4
HIDDEN = -1e30
VMEM = pl.BlockSpec(memory_space=pltpu.VMEM)
NT = (((1,), (1,)), ((), ()))
NN = (((1,), (0,)), ((), ()))


def rotated(shard, by):
    peers = lax.axis_size(AXES)
    return lax.ppermute(shard, AXES, [(i, (i + by) % peers) for i in range(peers)])


def swapped(shard):
    peers = lax.axis_size(AXES)
    return lax.ppermute(shard, AXES, [(i, i ^ 1) for i in range(peers)])


def dot(a, b, dims):
    return lax.dot_general(a, b, dims, preferred_element_type=jnp.float32)


def call(body, outs, args, scratch=(), cost=None, mib=24):
    return pl.pallas_call(
        body,
        out_shape=outs,
        in_specs=[VMEM] * len(args),
        out_specs=jax.tree.map(lambda _: VMEM, outs),
        scratch_shapes=list(scratch),
        compiler_params=pltpu.CompilerParams(vmem_limit_bytes=mib << 20),
        cost_estimate=pl.CostEstimate(flops=cost or 0, bytes_accessed=1 << 20, transcendentals=0),
    )(*args)


def pack_body(k_ref, v_ref, kv_ref):
    heads = k_ref.shape[1]
    for c in range(heads):
        kv_ref[c] = k_ref[:, c, :]
        kv_ref[heads + c] = v_ref[:, c, :]


def prepare_body(q_ref, g_ref, kv_ref, edges_ref, qr_ref, gr_ref, bias_ref, s_ref, w_ref):
    rows, heads, depth = q_ref.shape
    kv_heads = kv_ref.shape[0] // 2
    group = heads // kv_heads
    lanes = rows * group
    for c in range(kv_heads):
        own = slice(c * group, (c + 1) * group)
        qr_ref[c] = q_ref[:, own, :].astype(jnp.float32).reshape(lanes, depth).astype(jnp.bfloat16)
        gr_ref[c] = g_ref[:, own, :].astype(jnp.float32).reshape(lanes, depth).astype(jnp.bfloat16)
        s_ref[c] = dot(kv_ref[c], qr_ref[c], NT)
        w_ref[c] = dot(kv_ref[kv_heads + c], gr_ref[c], NT)
    local = lax.broadcasted_iota(jnp.int32, (rows, lanes), 0)
    token = lax.broadcasted_iota(jnp.int32, (rows, lanes), 1) // group
    start, low, high = edges_ref[0:1, :], edges_ref[1:2, :], edges_ref[2:3, :]
    for o in range(SPAN):
        if o == 0:
            key = jnp.where(local <= token, local, local - SPAN * rows)
        else:
            key = local - o * rows
        seen = (key >= start) & ((key < low) | (key >= high))
        bias_ref[o] = jnp.where(seen, 0.0, HIDDEN)


def main_body(*refs):
    kv_refs, (qr_ref, gr_ref, bias_ref, s_ref, w_ref), outs = refs[:SPAN], refs[SPAN : SPAN + 5], refs[SPAN + 5 :]
    part_refs, (ds_ref, p_ref, pm_ref) = outs[:SPAN], outs[SPAN:]
    kv_heads, lanes, depth = qr_ref.shape
    rows = s_ref.shape[1]
    scale = depth ** -0.5
    width = 256
    group = lanes // rows
    for c in range(kv_heads):
        for n in range(lanes // width):
            cols = slice(n * width, (n + 1) * width)
            q = qr_ref[c, cols, :]
            g = gr_ref[c, cols, :]
            local = lax.broadcasted_iota(jnp.int32, (rows, width), 0)
            token = lax.broadcasted_iota(jnp.int32, (rows, width), 1) // group + n * (width // group)
            inside = local <= token
            scores, weighs = [], []
            for o in range(SPAN):
                kv_ref = kv_refs[(o - 1) % SPAN]
                s = dot(kv_ref[c], q, NT)
                w = dot(kv_ref[kv_heads + c], g, NT)
                if o == 0:
                    s = jnp.where(inside, s_ref[c, :, cols], s)
                    w = jnp.where(inside, w_ref[c, :, cols], w)
                scores.append(s + bias_ref[o, :, cols])
                weighs.append(w)
            top = jnp.max(jnp.maximum(jnp.maximum(scores[0], scores[1]), jnp.maximum(scores[2], scores[3])), axis=0, keepdims=True)
            raw = [jnp.exp2((s - top) * (scale * math.log2(math.e))) for s in scores]
            total = jnp.sum(sum(raw), axis=0, keepdims=True)
            inverse = 1.0 / total
            delta = jnp.sum(sum(e * w for e, w in zip(raw, weighs)), axis=0, keepdims=True) * inverse
            for o in range(SPAN):
                prob = raw[o] * inverse
                dscore = (prob * scale) * (weighs[o] - delta)
                if o == 0:
                    p_ref[c, :, cols] = jnp.where(inside, prob, 0.0).astype(jnp.bfloat16)
                    ds_ref[c, SPAN * rows :, cols] = jnp.where(inside, dscore, 0.0).astype(jnp.bfloat16)
                    prob = jnp.where(inside, 0.0, prob)
                    dscore = jnp.where(inside, 0.0, dscore)
                at = slice(((o - 1) % SPAN) * rows, ((o - 1) % SPAN + 1) * rows)
                pm_ref[at, cols] = prob.astype(jnp.bfloat16)
                ds_ref[c, at, cols] = dscore.astype(jnp.bfloat16)
        dk = dot(ds_ref[c, : SPAN * rows, :], qr_ref[c], NN).astype(jnp.bfloat16)
        dv = dot(pm_ref[...], gr_ref[c], NN).astype(jnp.bfloat16)
        for o in range(SPAN):
            part_refs[o][c] = dk[o * rows : (o + 1) * rows]
            part_refs[o][kv_heads + c] = dv[o * rows : (o + 1) * rows]


def query_body(*refs):
    kv_refs, (ds_ref, p_ref, qr_ref, gr_ref), (dq_ref, own_ref, turned_ref) = refs[: SPAN + 1], refs[SPAN + 1 : SPAN + 5], refs[SPAN + 5 :]
    kv_heads, lanes, depth = qr_ref.shape
    rows = p_ref.shape[1]
    group = lanes // rows
    for c in range(kv_heads):
        own_ref[c] = dot(ds_ref[c, SPAN * rows :, :], qr_ref[c], NN)
        own_ref[kv_heads + c] = dot(p_ref[c], gr_ref[c], NN)
        for o in range(SPAN + 1):
            turned_ref[:, o * rows : (o + 1) * rows] = kv_refs[o][c].astype(jnp.float32).T.astype(jnp.bfloat16)
        dq = dot(turned_ref[...], ds_ref[c], NN).T
        dq_ref[:, c * group : (c + 1) * group, :] = dq.reshape(rows, group, depth).astype(jnp.bfloat16)


def finish_body(own_ref, near_ref, far_ref, dk_ref, dv_ref):
    kv_heads = own_ref.shape[0] // 2
    for c in range(kv_heads):
        for out_ref, at in ((dk_ref, c), (dv_ref, kv_heads + c)):
            total = own_ref[at] + near_ref[at].astype(jnp.float32) + far_ref[at].astype(jnp.float32)
            out_ref[:, c, :] = total.astype(jnp.bfloat16)


def per_device(queries, key_states, value_states, out_grad, bounds):
    rows, heads, depth = queries.shape
    kv_heads = key_states.shape[1]
    group = heads // kv_heads
    lanes = rows * group
    bf, f32 = jnp.bfloat16, jnp.float32
    shape = jax.ShapeDtypeStruct
    my_index = lax.axis_index(AXES)
    odd = lax.rem(my_index, 2) == 1
    product = 2 * kv_heads * rows * lanes * depth

    own = call(pack_body, shape((2 * kv_heads, rows, depth), bf), (key_states, value_states))
    far = rotated(own, 4)
    near = rotated(own, 2)
    edges = jnp.repeat(bounds - my_index * rows, group, axis=1)
    qr, gr, bias, s_own, w_own = call(
        prepare_body,
        (
            shape((kv_heads, lanes, depth), bf),
            shape((kv_heads, lanes, depth), bf),
            shape((SPAN, rows, lanes), f32),
            shape((kv_heads, rows, lanes), f32),
            shape((kv_heads, rows, lanes), f32),
        ),
        (queries, out_grad, own, edges),
        cost=2 * product,
    )
    one = swapped(jnp.where(odd, near, own))
    three = swapped(jnp.where(odd, far, near))
    block = shape((2 * kv_heads, rows, depth), bf)
    g1, g2, g3, g4, dscore, p_own = call(
        main_body,
        (block,) * SPAN + (shape((kv_heads, (SPAN + 1) * rows, lanes), bf), shape((kv_heads, rows, lanes), bf)),
        (one, near, three, far, qr, gr, bias, s_own, w_own),
        scratch=(pltpu.VMEM((SPAN * rows, lanes), bf),),
        cost=16 * product,
        mib=40,
    )
    b1 = swapped(g1)
    b3 = swapped(g3)
    dq, own_sum = call(
        query_body,
        (shape((rows, heads, depth), bf), shape((2 * kv_heads, rows, depth), f32)),
        (one, near, three, far, own, dscore, p_own, qr, gr),
        scratch=(pltpu.VMEM((depth, (SPAN + 1) * rows), bf),),
        cost=7 * product,
        mib=32,
    )
    b1, b3, g2, g4 = (x.astype(f32) for x in (b1, b3, g2, g4))
    zero = jnp.zeros_like(b1)
    to_near = (g2 + jnp.where(odd, b1, b3)).astype(bf)
    to_far = (g4 + jnp.where(odd, b3, zero)).astype(bf)
    from_far = rotated(to_far, -4)
    from_near = rotated(to_near, -2)
    own_sum = own_sum + jnp.where(odd, zero, b1)
    dk, dv = call(finish_body, (shape(key_states.shape, bf), shape(value_states.shape, bf)), (own_sum, from_near, from_far))
    return dq, dk, dv


def solution(mesh):
    rows = P(AXES, None, None)
    return jax.shard_map(
        per_device,
        mesh=mesh,
        in_specs=(rows, rows, rows, rows, P(None, AXES)),
        out_specs=(rows, rows, rows),
        check_vma=False,
    )
```

time: 89.7 us -> 58.3 us (0.65)
  the two profiles are of different devices: /device:TPU:27 before, /device:TPU:0 now
where the time goes in v1:
time: 58.3 us; the launch traced here: 58 us
  waiting for transfers between devices  25.8 us (44%)
  Pallas kernels  17.2 us (30%)
  starting transfers between devices  6.44 us (11%)
  local copies, waits for them, and re-layouts  6.24 us (11%)
  other arithmetic  1.74 us (3%)
  between operations  0.71 us (1%)
    ppermute x4, waiting for transfers between devices, rotated(): lax.ppermute(shard, AXES, [(i, (i + by) % peers) for i in range(peers)])  25.7 us
    pallas_call x5, Pallas kernels, call(): pl.pallas_call(body, out_shape=outs, in_specs=[VMEM] * len(args), out_spe...  17.2 us
    ppermute x4, starting transfers between devices, rotated(): lax.ppermute(shard, AXES, [(i, (i + by) % peers) for i in range(peers)])  5.42 us
    unnamed x10, local copies, waits for them, and re-layouts  4.38 us
  transfers between devices with their start and end apart: 8, of which 4 were waited for; matrix products, arithmetic and copies ran while one was open for 4% of the time, Pallas kernels for 7%

profile of v1, /device:TPU:0, one launch (start us, length us, event | category | flops | bytes accessed | tf_op | source)
XLA Modules:
  0.0 58.0 jit_solution(16832527682624680757)
XLA Ops:
  0.6 0.0 copy-start.2
  0.6 0.0 copy-start.3
  0.7 1.0 %copy-done.3 = bf16[128,4,128]{2,1,0:T(4,128)(2,1)S(1)} copy-done((bf16[128,4,128]{2,1,0:T(4,128)(2,1)S(1)}, bf16[128,4,128]{2,1,0:T(4,128)(2,1)}, u32[]{:S(2)}) %copy-start.3) | copy-done | bytes 131096
  1.6 0.9 %copy-done.4 = bf16[128,4,128]{2,1,0:T(4,128)(2,1)S(1)} copy-done((bf16[128,4,128]{2,1,0:T(4,128)(2,1)S(1)}, bf16[128,4,128]{2,1,0:T(4,128)(2,1)}, u32[]{:S(2)}) %copy-start.4) | copy-done | bytes 131096
  2.5 0.6 %shard_map.76.kv_ref.refs_4_ = bf16[8,128,128]{2,1,0:T(8,128)(2,1)S(1)} custom-call(bf16[128,4,128]{2,1,0:T(4,128)(2,1)S(1)} %copy-done.3, bf16[128,4,128]{2,1,0:T(4,128)(2,1)S(1)} %copy-done.4), custom_call_target="tpu_custom_call" | custom-call | bytes 1048576 | tf_op jit(solution)/shard_map/pallas_call | solution.py:33
  3.2 3.0 %collective-permute-start.2 = (bf16[8,128,128]{2,1,0:T(8,128)(2,1)S(1)}, bf16[8,128,128]{2,1,0:T(8,128)(2,1)S(1)}, u32[]{:S(2)}, u32[]{:S(2)}) collective-permute-start(bf16[8,128,128]{2,1,0:T(8,128)(2,1)S(1)} %shard_map.76.kv_ref.refs_4_), channel_id=1, source_target_pairs={{0,4},{1,5},{2,6},{3,7},{4,8},{5,9},{6,10},{7,11},{8,12},{9,13},{1... | collective-permute-start | bytes 786440 | tf_op jit(solution)/shard_map/ppermute | solution.py:20
  6.2 1.5 %collective-permute-start = (bf16[8,128,128]{2,1,0:T(8,128)(2,1)S(1)}, bf16[8,128,128]{2,1,0:T(8,128)(2,1)S(1)}, u32[]{:S(2)}, u32[]{:S(2)}) collective-permute-start(bf16[8,128,128]{2,1,0:T(8,128)(2,1)S(1)} %shard_map.76.kv_ref.refs_4_), channel_id=1, source_target_pairs={{0,2},{1,3},{2,4},{3,5},{4,6},{5,7},{6,8},{7,9},{8,10},{9,11},{10,... | collective-permute-start | bytes 786440 | tf_op jit(solution)/shard_map/ppermute | solution.py:20
  7.7 9.7 %collective-permute-done.2.refs_3_ = bf16[8,128,128]{2,1,0:T(8,128)(2,1)S(1)} collective-permute-done((bf16[8,128,128]{2,1,0:T(8,128)(2,1)S(1)}, bf16[8,128,128]{2,1,0:T(8,128)(2,1)S(1)}, u32[]{:S(2)}, u32[]{:S(2)}) %collective-permute-start.2) | collective-permute-done | bytes 262176 | tf_op jit(solution)/shard_map/ppermute | solution.py:20
  17.4 4.7 %collective-permute-done.refs_1_ = bf16[8,128,128]{2,1,0:T(8,128)(2,1)S(1)} collective-permute-done((bf16[8,128,128]{2,1,0:T(8,128)(2,1)S(1)}, bf16[8,128,128]{2,1,0:T(8,128)(2,1)S(1)}, u32[]{:S(2)}, u32[]{:S(2)}) %collective-permute-start) | collective-permute-done | bytes 262176 | tf_op jit(solution)/shard_map/ppermute | solution.py:20
  22.1 0.8 %broadcast_select_fusion = (bf16[8,128,128]{2,1,0:T(8,128)(2,1)}, bf16[8,128,128]{2,1,0:T(8,128)(2,1)}) fusion(bf16[8,128,128]{2,1,0:T(8,128)(2,1)S(1)} %collective-permute-done.2.refs_3_, bf16[8,128,128]{2,1,0:T(8,128)(2,1)S(1)} %collective-permute-done.refs_1_, pred[]{:T(512)S(6)} %eq.3, bf16[8,128,128]{2,1,0:T(8,128)(2,1)S(1)} %shard_map.76.kv_ref.refs_4_), kind=kLoop, calls=%fused_computation.8 | loop fusion | flops 262144 | bytes 1310721 | tf_op jit(solution)/shard_map/jit(_where)/select_n | solution.py:173
  22.9 0.0 collective-permute-start.3
  22.9 0.5 collective-permute-start.1
  23.4 0.7 %broadcast_subtract_fusion = s32[3,128]{1,0:T(4,128)S(1)} fusion(s32[3,128]{1,0:T(4,128)} %param.9, s32[]{:T(128)S(6)} %mul.7), kind=kLoop, calls=%fused_computation.10 | loop fusion | flops 384 | bytes 3076 | tf_op jit(solution)/shard_map/sub | solution.py:159
  24.1 0.8 %broadcast_in_dim.6 = s32[3,128,8]{2,1,0:T(8,128)} broadcast(s32[3,128]{1,0:T(4,128)S(1)} %broadcast_subtract_fusion), dimensions={0,1} | broadcast | bytes 13824 | tf_op jit(solution)/shard_map/broadcast_in_dim | solution.py:159
  24.9 1.1 %reshape.9.edges_ref = s32[3,1024]{1,0:T(4,128)S(1)} reshape(s32[3,128,8]{2,1,0:T(8,128)} %broadcast_in_dim.6) | data formatting | bytes 24576 | tf_op jit(solution)/shard_map/reshape | solution.py:159
  26.0 0.0 copy-done.2
  26.0 1.5 %shard_map.77 = (bf16[4,1024,128]{2,1,0:T(8,128)(2,1)S(1)}, bf16[4,1024,128]{2,1,0:T(8,128)(2,1)S(1)}, f32[4,128,1024]{2,1,0:T(8,128)S(1)}, f32[4,128,1024]{2,1,0:T(8,128)S(1)}, f32[4,128,1024]{2,1,0:T(8,128)S(1)}) custom-call(bf16[128,32,128]{2,1,0:T(8,128)(2,1)S(1)} %copy-done.1, bf16[128,32,128]{2,1,0:T(8,128)(2,1)S(1)} %copy-done.2, ...), custom_call_target="tpu_custom_call" | custom-call | flops 268435456 | bytes 1048576 | tf_op jit(solution)/shard_map/pallas_call | solution.py:33
  27.5 0.0 collective-permute-done.3.refs_2_
  27.5 0.0 collective-permute-done.1.refs_0_
  27.5 10.7 %shard_map.78 = (bf16[8,128,128]{2,1,0:T(8,128)(2,1)S(1)}, bf16[8,128,128]{2,1,0:T(8,128)(2,1)S(1)}, bf16[8,128,128]{2,1,0:T(8,128)(2,1)S(1)}, bf16[8,128,128]{2...) custom-call(bf16[8,128,128]{2,1,0:T(8,128)(2,1)S(1)} %collective-permute-done.1.refs_0_, ...), custom_call_target="tpu_custom_call" | custom-call | flops 2147483648 | bytes 1048576 | tf_op jit(solution)/shard_map/pallas_call | solution.py:33
  38.2 0.0 collective-permute-start.4
  38.2 0.5 collective-permute-start.5
  38.7 2.5 %copy-done = bf16[4,640,1024]{2,1,0:T(8,128)(2,1)S(1)} copy-done((bf16[4,640,1024]{2,1,0:T(8,128)(2,1)S(1)}, bf16[4,640,1024]{2,1,0:T(8,128)(2,1)}, u32[]{:S(2)}) %copy-start) | copy-done | bytes 5242904
  41.2 2.6 %shard_map.79 = (bf16[128,32,128]{2,1,0:T(8,128)(2,1)}, f32[8,128,128]{2,1,0:T(8,128)S(1)}) custom-call(bf16[8,128,128]{2,1,0:T(8,128)(2,1)S(1)} %collective-permute-done.1.refs_0_, bf16[8,128,128]{2,1,0:T(8,128)(2,1)S(1)} %collective-permute-done.refs_1_, bf16[8,128,128]{2,1,0:T(8,128)(2,1)S(1)} %collective-permute-done.3.refs_2_, ...), custom_call_target="tpu_custom_call" | custom-call | flops 939524096 | bytes 1048576 | tf_op jit(solution)/shard_map/pallas_call | solution.py:33
  43.8 0.0 collective-permute-done.4
  43.8 0.0 collective-permute-done.5
  43.8 0.2 fusion.4
  44.0 0.9 %collective-permute-start.7 = (bf16[8,128,128]{2,1,0:T(8,128)(2,1)S(1)}, bf16[8,128,128]{2,1,0:T(8,128)(2,1)S(1)}, u32[]{:S(2)}, u32[]{:S(2)}) collective-permute-start(bf16[8,128,128]{2,1,0:T(8,128)(2,1)S(1)} %get-tuple-element.33), channel_id=1, source_target_pairs={{0,28},{1,29},{2,30},{3,31},{4,0},{5,1},{6,2},{7,3},{8,4},{9,5},{1... | collective-permute-start | bytes 786440 | tf_op jit(solution)/shard_map/ppermute | solution.py:20
  44.9 0.0 collective-permute-start.6
  44.9 7.4 %collective-permute-done.7.far_ref = bf16[8,128,128]{2,1,0:T(8,128)(2,1)S(1)} collective-permute-done((bf16[8,128,128]{2,1,0:T(8,128)(2,1)S(1)}, bf16[8,128,128]{2,1,0:T(8,128)(2,1)S(1)}, u32[]{:S(2)}, u32[]{:S(2)}) %collective-permute-start.7) | collective-permute-done | bytes 262176 | tf_op jit(solution)/shard_map/ppermute | solution.py:20
  52.3 4.0 %collective-permute-done.6.near_ref = bf16[8,128,128]{2,1,0:T(8,128)(2,1)S(1)} collective-permute-done((bf16[8,128,128]{2,1,0:T(8,128)(2,1)S(1)}, bf16[8,128,128]{2,1,0:T(8,128)(2,1)S(1)}, u32[]{:S(2)}, u32[]{:S(2)}) %collective-permute-start.6) | collective-permute-done | bytes 262176 | tf_op jit(solution)/shard_map/ppermute | solution.py:20
  56.3 1.8 %shard_map.80 = (bf16[128,4,128]{2,1,0:T(4,128)(2,1)}, bf16[128,4,128]{2,1,0:T(4,128)(2,1)}) custom-call(f32[8,128,128]{2,1,0:T(8,128)S(1)} %get-tuple-element.35.own_ref, bf16[8,128,128]{2,1,0:T(8,128)(2,1)S(1)} %collective-permute-done.6.near_ref, bf16[8,128,128]{2,1,0:T(8,128)(2,1)S(1)} %collective-permute-done.7.far_ref), custom_call_target="tpu_custom_call" | custom-call | bytes 1048576 | tf_op jit(solution)/shard_map/pallas_call | solution.py:33
  (4 shorter events, 0.0 us)
Async XLA Ops:
  0.6 25.4 %copy-start.2 = (bf16[128,32,128]{2,1,0:T(8,128)(2,1)S(1)}, bf16[128,32,128]{2,1,0:T(8,128)(2,1)}, u32[]{:S(2)}) copy-start(bf16[128,32,128]{2,1,0:T(8,128)(2,1)} %g_ref.1) | copy-start | bytes 3145732
  0.6 1.0 %copy-start.3 = (bf16[128,4,128]{2,1,0:T(4,128)(2,1)S(1)}, bf16[128,4,128]{2,1,0:T(4,128)(2,1)}, u32[]{:S(2)}) copy-start(bf16[128,4,128]{2,1,0:T(4,128)(2,1)} %k_ref.1) | copy-start | bytes 393220
  1.6 0.9 %copy-start.4 = (bf16[128,4,128]{2,1,0:T(4,128)(2,1)S(1)}, bf16[128,4,128]{2,1,0:T(4,128)(2,1)}, u32[]{:S(2)}) copy-start(bf16[128,4,128]{2,1,0:T(4,128)(2,1)} %v_ref.1) | copy-start | bytes 393220
  2.5 23.5 %copy-start.1 = (bf16[128,32,128]{2,1,0:T(8,128)(2,1)S(1)}, bf16[128,32,128]{2,1,0:T(8,128)(2,1)}, u32[]{:S(2)}) copy-start(bf16[128,32,128]{2,1,0:T(8,128)(2,1)} %q_ref.1) | copy-start | bytes 3145732
  3.2 14.2 %collective-permute-start.2 = (bf16[8,128,128]{2,1,0:T(8,128)(2,1)S(1)}, bf16[8,128,128]{2,1,0:T(8,128)(2,1)S(1)}, u32[]{:S(2)}, u32[]{:S(2)}) collective-permute-start(bf16[8,128,128]{2,1,0:T(8,128)(2,1)S(1)} %shard_map.76.kv_ref.refs_4_), channel_id=1, source_target_pairs={{0,4},{1,5},{2,6},{3,7},{4,8},{5,9},{6,10},{7,11},{8,12},{9,13},{1... | collective-permute-start | bytes 786440 | tf_op jit(solution)/shard_map/ppermute | solution.py:20
  6.2 15.9 %collective-permute-start = (bf16[8,128,128]{2,1,0:T(8,128)(2,1)S(1)}, bf16[8,128,128]{2,1,0:T(8,128)(2,1)S(1)}, u32[]{:S(2)}, u32[]{:S(2)}) collective-permute-start(bf16[8,128,128]{2,1,0:T(8,128)(2,1)S(1)} %shard_map.76.kv_ref.refs_4_), channel_id=1, source_target_pairs={{0,2},{1,3},{2,4},{3,5},{4,6},{5,7},{6,8},{7,9},{8,10},{9,11},{10,... | collective-permute-start | bytes 786440 | tf_op jit(solution)/shard_map/ppermute | solution.py:20
  22.9 4.6 %collective-permute-start.3 = (bf16[8,128,128]{2,1,0:T(8,128)(2,1)}, bf16[8,128,128]{2,1,0:T(8,128)(2,1)S(1)}, u32[]{:S(2)}, u32[]{:S(2)}) collective-permute-start(bf16[8,128,128]{2,1,0:T(8,128)(2,1)} %get-tuple-element.36), channel_id=1, source_target_pairs={{0,1},{1,0},{2,3},{3,2},{4,5},{5,4},{6,7},{7,6},{8,9},{9,8},{10,11... | collective-permute-start | bytes 786440 | tf_op jit(solution)/shard_map/ppermute | solution.py:25
  22.9 4.6 %collective-permute-start.1 = (bf16[8,128,128]{2,1,0:T(8,128)(2,1)}, bf16[8,128,128]{2,1,0:T(8,128)(2,1)S(1)}, u32[]{:S(2)}, u32[]{:S(2)}) collective-permute-start(bf16[8,128,128]{2,1,0:T(8,128)(2,1)} %get-tuple-element.37), channel_id=1, source_target_pairs={{0,1},{1,0},{2,3},{3,2},{4,5},{5,4},{6,7},{7,6},{8,9},{9,8},{10,11... | collective-permute-start | bytes 786440 | tf_op jit(solution)/shard_map/ppermute | solution.py:25
  38.2 5.6 %collective-permute-start.4 = (bf16[8,128,128]{2,1,0:T(8,128)(2,1)S(1)}, bf16[8,128,128]{2,1,0:T(8,128)(2,1)S(1)}, u32[]{:S(2)}, u32[]{:S(2)}) collective-permute-start(bf16[8,128,128]{2,1,0:T(8,128)(2,1)S(1)} %get-tuple-element.27), channel_id=1, source_target_pairs={{0,1},{1,0},{2,3},{3,2},{4,5},{5,4},{6,7},{7,6},{8,9},{9,8},{10,11... | collective-permute-start | bytes 786440 | tf_op jit(solution)/shard_map/ppermute | solution.py:25
  38.2 5.6 %collective-permute-start.5 = (bf16[8,128,128]{2,1,0:T(8,128)(2,1)S(1)}, bf16[8,128,128]{2,1,0:T(8,128)(2,1)S(1)}, u32[]{:S(2)}, u32[]{:S(2)}) collective-permute-start(bf16[8,128,128]{2,1,0:T(8,128)(2,1)S(1)} %get-tuple-element.29), channel_id=1, source_target_pairs={{0,1},{1,0},{2,3},{3,2},{4,5},{5,4},{6,7},{7,6},{8,9},{9,8},{10,11... | collective-permute-start | bytes 786440 | tf_op jit(solution)/shard_map/ppermute | solution.py:25
  38.7 2.5 %copy-start = (bf16[4,640,1024]{2,1,0:T(8,128)(2,1)S(1)}, bf16[4,640,1024]{2,1,0:T(8,128)(2,1)}, u32[]{:S(2)}) copy-start(bf16[4,640,1024]{2,1,0:T(8,128)(2,1)} %get-tuple-element.23.refs_5_) | copy-start | bytes 15728644
  44.0 8.3 %collective-permute-start.7 = (bf16[8,128,128]{2,1,0:T(8,128)(2,1)S(1)}, bf16[8,128,128]{2,1,0:T(8,128)(2,1)S(1)}, u32[]{:S(2)}, u32[]{:S(2)}) collective-permute-start(bf16[8,128,128]{2,1,0:T(8,128)(2,1)S(1)} %get-tuple-element.33), channel_id=1, source_target_pairs={{0,28},{1,29},{2,30},{3,31},{4,0},{5,1},{6,2},{7,3},{8,4},{9,5},{1... | collective-permute-start | bytes 786440 | tf_op jit(solution)/shard_map/ppermute | solution.py:20
  44.9 11.4 %collective-permute-start.6 = (bf16[8,128,128]{2,1,0:T(8,128)(2,1)S(1)}, bf16[8,128,128]{2,1,0:T(8,128)(2,1)S(1)}, u32[]{:S(2)}, u32[]{:S(2)}) collective-permute-start(bf16[8,128,128]{2,1,0:T(8,128)(2,1)S(1)} %get-tuple-element.34), channel_id=1, source_target_pairs={{0,30},{1,31},{2,0},{3,1},{4,2},{5,3},{6,4},{7,5},{8,6},{9,7},{10,... | collective-permute-start | bytes 786440 | tf_op jit(solution)/shard_map/ppermute | solution.py:20
